TPU v7x, 32 devices: a whole 2x2x4 slice. The times are simulated.
32 devices in a mesh: dp: 16 (over z, y, x), mp: 2 (over core).
Axes of the slice: x: 2, y: 2, z: 4, core: 2. Of those that a mesh axis runs over, the one named last changes fastest.
Arguments:
- tokens: bfloat16 [32768, 768], P(('dp', 'mp')), may hold values from -6 to 6
- out_grad: bfloat16 [32768, 768], P(('dp', 'mp')), may hold values from -6 to 6
- image_lengths: int32 [16, 69], P('dp'), may hold values from 0 to 98, as said below
- group_of_block: int32 [16], P('dp'), may hold values from 0 to 2, as said below
- norm_gains: float32 [2, 768], replicated, may hold values from 0.5 to 1.5
- row_biases: float32 [4, 768], replicated, may hold values from -1.5 to 1.5
- w_qkv: bfloat16 [3, 768, 768], P(None, None, 'mp'), may hold values from -0.21875 to 0.21875
- qv_bias: float32 [2, 768], P(None, 'mp'), may hold values from -1.5 to 1.5
- w_out: bfloat16 [768, 768], P('mp'), may hold values from -0.875 to 0.875
- w_fc1: bfloat16 [768, 3072], P(None, 'mp'), may hold values from -0.21875 to 0.21875
- b_fc1: float32 [3072], P('mp'), may hold values from -1.5 to 1.5
- w_fc2: bfloat16 [3072, 768], P('mp'), may hold values from -0.109375 to 0.109375
Outputs:
- output: bfloat16 [32768, 768], P(('dp', 'mp'))
- tokens_grad: float32 [32768, 768], P(('dp', 'mp'))
- norm_gains_grad: float32 [2, 768], replicated
- row_biases_grad: float32 [4, 768], replicated
- w_qkv_grad: float32 [3, 768, 768], P(None, None, 'mp')
- qv_bias_grad: float32 [2, 768], P(None, 'mp')
- w_out_grad: float32 [768, 768], P('mp')
- w_fc1_grad: float32 [768, 3072], P(None, 'mp')
- b_fc1_grad: float32 [3072], P('mp')
- w_fc2_grad: float32 [3072, 768], P('mp')
Inputs may be any that keep to these rules, and one draw needn't show every extreme that they name: `image_lengths`: row b lists the patch counts of the images packed in block b from the first slot on; each image has 30 to 98 patches, slots after the last image hold 0, the counts of a row sum to at most 2048 and the rest of the block is padding; every block has an image of 98 patches. `group_of_block`: entry b is the dataset group of block b; it never falls along the blocks, and each of the 3 groups holds at least one block.
All inputs are finite; a program needn't handle non-finite values.
Results may differ from a plain program's by a relative error of at most 0.015.
Values may be sent and summed in bfloat16 or wider, within the bound.
No kernel may reach another device: no remote copies, remote signals or barrier semaphores. Data moves between devices by JAX's collectives and lax.ppermute only.
A program may use at most 256 MiB of HBM per device.

v0:
```python
import jax
import jax.numpy as jnp
from jax import lax
from jax.sharding import PartitionSpec as P

HEAD_DIM = 64
GROUPS = 3
LEN_NORM = 64


def layer_norm(values, gain_vec, shift_vec):
    center = values - jnp.mean(values, axis=-1, keepdims=True)
    spread = jnp.mean(center * center, axis=-1, keepdims=True)
    return center * lax.rsqrt(spread + 1e-06) * gain_vec + shift_vec


def gelu_tanh(values):
    return (
        0.5
        * values
        * (1.0 + jnp.tanh(0.7978845608028654 * (values + 0.044715 * values * values * values)))
    )


def image_rows(lengths, row_count):
    image_ends = jnp.cumsum(lengths)
    position = jnp.arange(row_count, dtype=jnp.int32)
    segment = jnp.sum((position[:, None] >= image_ends[None, :]).astype(jnp.int32), axis=1)
    slot_ids = jnp.arange(lengths.shape[0], dtype=jnp.int32)
    row_length = jnp.sum(
        jnp.where(segment[:, None] == slot_ids[None, :], lengths[None, :], 0), axis=1
    )
    return (segment, row_length)


def score_block(query_block, segment_block, keys_all, segment, score_scale):
    scores = (
        jnp.einsum("qhd,khd->hqk", query_block, keys_all, preferred_element_type=jnp.float32)
        * score_scale
    )
    return jnp.where((segment_block[:, None] == segment[None, :])[None], scores, -1000000000.0)


def local(
    tokens,
    out_grad,
    image_lengths,
    group_of_block,
    norm_gains,
    row_biases,
    w_qkv,
    qv_bias,
    w_out,
    w_fc1,
    b_fc1,
    w_fc2,
):
    own_rows = tokens.shape[0]
    row_count = own_rows * lax.axis_size("mp")
    first_row = lax.axis_index("mp") * own_rows
    segment, row_length = image_rows(image_lengths[0], row_count)
    images = jnp.sum((image_lengths[0] > 0).astype(jnp.float32))
    member = (group_of_block[0] == jnp.arange(GROUPS, dtype=jnp.int32)).astype(jnp.float32)
    group_images = lax.psum(member * images, "dp")
    group_roots = jnp.sqrt(group_images)
    factor = jnp.sum(group_images) / (group_roots * jnp.sum(group_roots))
    block_factor = jnp.sum(member * factor)
    own_length = lax.dynamic_slice_in_dim(row_length, first_row, own_rows)
    weight_row = (
        block_factor
        * LEN_NORM
        * (own_length > 0).astype(jnp.float32)
        / jnp.maximum(own_length, 1).astype(jnp.float32)
    )
    tokens_f = tokens.astype(jnp.float32)
    normed, norm_pull = jax.vjp(layer_norm, tokens_f, norm_gains[0], row_biases[0])
    normed_low = normed.astype(jnp.bfloat16)
    normed_all = lax.all_gather(normed_low, "mp", axis=0, tiled=True)
    projected = jnp.einsum("rd,tde->tre", normed_all, w_qkv, preferred_element_type=jnp.float32)
    bias_three = jnp.stack([qv_bias[0], jnp.zeros_like(qv_bias[0]), qv_bias[1]])
    projected = (projected + bias_three[:, None, :]).astype(jnp.bfloat16)
    local_width = w_qkv.shape[2]
    head_count = local_width // HEAD_DIM
    shaped = projected.reshape(3, row_count, head_count, HEAD_DIM)
    queries, keys_all, values_all = (shaped[0], shaped[1], shaped[2])
    block_rows = min(512, row_count)
    block_count = row_count // block_rows
    score_scale = HEAD_DIM ** (-0.5)
    query_blocks = queries.reshape(block_count, block_rows, head_count, HEAD_DIM)
    segment_blocks = segment.reshape(block_count, block_rows)

    def forward_block(pieces):
        query_block, segment_block = pieces
        scores = score_block(query_block, segment_block, keys_all, segment, score_scale)
        top_score = jnp.max(scores, axis=-1, keepdims=True)
        exponent = jnp.exp(scores - top_score)
        total = jnp.sum(exponent, axis=-1, keepdims=True)
        weights = (exponent / total).astype(jnp.bfloat16)
        context = jnp.einsum(
            "hqk,khd->qhd", weights, values_all, preferred_element_type=jnp.float32
        )
        return (context, (top_score + jnp.log(total))[:, :, 0])

    context, log_total = lax.map(forward_block, (query_blocks, segment_blocks))
    context_low = context.reshape(row_count, local_width).astype(jnp.bfloat16)
    piece = context_low
    attention = lax.psum_scatter(
        jnp.dot(piece, w_out, preferred_element_type=jnp.float32).astype(jnp.bfloat16),
        "mp",
        scatter_dimension=0,
        tiled=True,
    ).astype(jnp.float32)
    hidden_one = tokens_f + attention + row_biases[2]
    normed_two, norm_two_pull = jax.vjp(layer_norm, hidden_one, norm_gains[1], row_biases[1])
    normed_two_all = lax.all_gather(normed_two.astype(jnp.bfloat16), "mp", axis=0, tiled=True)
    before = jnp.dot(normed_two_all, w_fc1, preferred_element_type=jnp.float32) + b_fc1
    activated, gelu_pull = jax.vjp(gelu_tanh, before)
    activated_low = activated.astype(jnp.bfloat16)
    piece = activated_low
    mlp_out = lax.psum_scatter(
        jnp.dot(piece, w_fc2, preferred_element_type=jnp.float32).astype(jnp.bfloat16),
        "mp",
        scatter_dimension=0,
        tiled=True,
    ).astype(jnp.float32)
    output = (hidden_one + mlp_out + row_biases[3]).astype(jnp.bfloat16)
    out_cot = out_grad.astype(jnp.float32) * weight_row[:, None]
    out_cot_all = lax.all_gather(out_cot.astype(jnp.bfloat16), "mp", axis=0, tiled=True)
    grad_fc2 = jnp.einsum(
        "rf,rd->fd", activated_low, out_cot_all, preferred_element_type=jnp.float32
    )
    grad_act = jnp.einsum("rd,fd->rf", out_cot_all, w_fc2, preferred_element_type=jnp.float32)
    grad_before = gelu_pull(grad_act)[0].astype(jnp.bfloat16)
    grad_bfc1 = jnp.sum(grad_before.astype(jnp.float32), axis=0)
    grad_fc1 = jnp.einsum(
        "rd,rf->df", normed_two_all, grad_before, preferred_element_type=jnp.float32
    )
    piece = grad_before
    grad_norm_two = lax.psum_scatter(
        jnp.einsum("rf,df->rd", piece, w_fc1, preferred_element_type=jnp.float32).astype(
            jnp.bfloat16
        ),
        "mp",
        scatter_dimension=0,
        tiled=True,
    ).astype(jnp.float32)
    grad_hidden, grad_gain_two, grad_shift_two = norm_two_pull(grad_norm_two)
    grad_hidden = grad_hidden + out_cot
    grad_hidden_all = lax.all_gather(grad_hidden.astype(jnp.bfloat16), "mp", axis=0, tiled=True)
    grad_out = jnp.einsum(
        "rc,rd->cd", context_low, grad_hidden_all, preferred_element_type=jnp.float32
    )
    grad_context = jnp.einsum(
        "rd,cd->rc", grad_hidden_all, w_out, preferred_element_type=jnp.float32
    ).astype(jnp.bfloat16)
    context_blocks = grad_context.reshape(block_count, block_rows, head_count, HEAD_DIM)

    def backward_block(carry, pieces):
        grad_keys, grad_values = carry
        query_block, segment_block, log_block, grad_block = pieces
        scores = score_block(query_block, segment_block, keys_all, segment, score_scale)
        probs = jnp.exp(scores - log_block[:, :, None])
        grad_values = grad_values + jnp.einsum(
            "hqk,qhd->khd",
            probs.astype(jnp.bfloat16),
            grad_block,
            preferred_element_type=jnp.float32,
        )
        grad_probs = jnp.einsum(
            "qhd,khd->hqk", grad_block, values_all, preferred_element_type=jnp.float32
        )
        grad_scores = probs * (grad_probs - jnp.sum(probs * grad_probs, axis=-1, keepdims=True))
        grad_scores = grad_scores.astype(jnp.bfloat16)
        grad_query = (
            jnp.einsum("hqk,khd->qhd", grad_scores, keys_all, preferred_element_type=jnp.float32)
            * score_scale
        )
        grad_keys = (
            grad_keys
            + jnp.einsum(
                "hqk,qhd->khd", grad_scores, query_block, preferred_element_type=jnp.float32
            )
            * score_scale
        )
        return ((grad_keys, grad_values), grad_query)

    zero_heads = jnp.zeros((row_count, head_count, HEAD_DIM), jnp.float32)
    (grad_keys, grad_values), grad_queries = lax.scan(
        backward_block,
        (zero_heads, zero_heads),
        (query_blocks, segment_blocks, log_total, context_blocks),
    )
    grad_projected = jnp.stack(
        [
            grad_queries.reshape(row_count, local_width),
            grad_keys.reshape(row_count, local_width),
            grad_values.reshape(row_count, local_width),
        ]
    ).astype(jnp.bfloat16)
    grad_qv_bias = jnp.stack(
        [
            jnp.sum(grad_projected[0].astype(jnp.float32), axis=0),
            jnp.sum(grad_projected[2].astype(jnp.float32), axis=0),
        ]
    )
    grad_qkv = jnp.einsum(
        "rd,tre->tde", normed_all, grad_projected, preferred_element_type=jnp.float32
    )
    piece = grad_projected
    grad_norm_one = lax.psum_scatter(
        jnp.einsum("tre,tde->rd", piece, w_qkv, preferred_element_type=jnp.float32).astype(
            jnp.bfloat16
        ),
        "mp",
        scatter_dimension=0,
        tiled=True,
    ).astype(jnp.float32)
    grad_input, grad_gain_one, grad_shift_one = norm_pull(grad_norm_one)
    grad_input = grad_input + grad_hidden
    gain_grads, shift_grads = lax.psum(
        (
            jnp.stack([grad_gain_one, grad_gain_two]),
            jnp.stack(
                [
                    grad_shift_one,
                    grad_shift_two,
                    jnp.sum(grad_hidden, axis=0),
                    jnp.sum(out_cot, axis=0),
                ]
            ),
        ),
        ("dp", "mp"),
    )
    grad_qkv, grad_qv_bias, grad_out, grad_fc1, grad_bfc1, grad_fc2 = lax.psum(
        (grad_qkv, grad_qv_bias, grad_out, grad_fc1, grad_bfc1, grad_fc2), "dp"
    )
    return (
        output,
        grad_input,
        gain_grads,
        shift_grads,
        grad_qkv,
        grad_qv_bias,
        grad_out,
        grad_fc1,
        grad_bfc1,
        grad_fc2,
    )


def solution(mesh):
    placed = (
        P(("dp", "mp"), None),
        P(("dp", "mp"), None),
        P("dp", None),
        P("dp"),
        P(),
        P(),
        P(None, None, "mp"),
        P(None, "mp"),
        P("mp", None),
        P(None, "mp"),
        P("mp"),
        P("mp", None),
    )
    return jax.shard_map(
        local,
        mesh=mesh,
        in_specs=placed,
        out_specs=(
            P(("dp", "mp"), None),
            P(("dp", "mp"), None),
            P(),
            P(),
            P(None, None, "mp"),
            P(None, "mp"),
            P("mp", None),
            P(None, "mp"),
            P("mp"),
            P("mp", None),
        ),
        check_vma=False,
    )
```

profile of v0, /device:TPU:0, one launch (start us, length us, event | category | flops | bytes accessed | tf_op | source)
XLA Modules:
  0.0 1192.0 jit_solution(15143467741998065962)
XLA Ops:
  15.6 14.2 %all-gather.5.cloned.1.call-done = bf16[2048,768]{1,0:T(8,128)(2,1)} async-done(((bf16[1024,768]{1,0:T(8,128)(2,1)}), bf16[2048,768]{1,0:T(8,128)(2,1)}) %all-gather.5.cloned.1.call-update) | async-done | bytes 3145744 | tf_op jit(solution)/shard_map/all_gather | solution.py:78
  29.8 6.3 fusion.45
  38.5 4.0 reshape_squeeze.3
  46.7 159.6 %while.27 = (s32[]{:T(128)}, bf16[4,512,6,64]{1,3,2,0:T(8,128)(2,1)}, f32[4,6,512]{2,1,0:T(8,128)S(1)}, s32[4,512]{1,0:T(4,128)S(1)}, s32[2048]{0:T(1024)S(1)}, ...) while((s32[]{:T(128)}, ...), condition=%wide.region_7.8_spmd, body=%wide.region_4.7_spmd.sunk | while | flops 1687155712 | bytes 103024832 | solution.py:104
  47.3 14.3 %fusion.128 = (f32[6,512]{1,0:T(8,128)S(1)}, f32[6,512,2048]{2,1,0:T(8,128)}) fusion(pred[512,2048]{1,0:T(8,128)(4,1)S(1)} %broadcast_compare_fusion.4, bf16[2048,6,64]{0,2,1:T(8,128)(2,1)} %get-tuple-element.469, bf16[4,512,6,64]{1,3,2,0:T(8,128)(2,1)} %get-tuple-element.468, s32[]{:T(128)S(6)} %copy.67), kind=kOutput, calls=%fused_computation.3.clone.1 | convolution fusion | flops 824177664 | bytes 28192772 | tf_op jit(solution)/shard_map/while/body/eval_jaxpr/qhd,khd->hqk/dot_general | solution.py:38
  61.6 12.1 %fusion.129 = f32[6,512]{1,0:T(8,128)S(1)} fusion(f32[6,512,2048]{2,1,0:T(8,128)} %get-tuple-element.430, f32[6,512]{1,0:T(8,128)S(1)} %get-tuple-element.431, pred[512,2048]{1,0:T(8,128)(4,1)S(1)} %broadcast_compare_fusion.4), kind=kLoop, calls=%fused_computation.4.clone.1 | loop fusion | flops 25162752 | bytes 26238976 | tf_op jit(solution)/shard_map/while/body/eval_jaxpr/reduce_sum | solution.py:97
  73.7 11.6 fusion.130
  87.2 14.3 %fusion.128 = (f32[6,512]{1,0:T(8,128)S(1)}, f32[6,512,2048]{2,1,0:T(8,128)}) fusion(pred[512,2048]{1,0:T(8,128)(4,1)S(1)} %broadcast_compare_fusion.4, bf16[2048,6,64]{0,2,1:T(8,128)(2,1)} %get-tuple-element.469, bf16[4,512,6,64]{1,3,2,0:T(8,128)(2,1)} %get-tuple-element.468, s32[]{:T(128)S(6)} %copy.67), kind=kOutput, calls=%fused_computation.3.clone.1 | convolution fusion | flops 824177664 | bytes 28192772 | tf_op jit(solution)/shard_map/while/body/eval_jaxpr/qhd,khd->hqk/dot_general | solution.py:38
  101.5 12.1 %fusion.129 = f32[6,512]{1,0:T(8,128)S(1)} fusion(f32[6,512,2048]{2,1,0:T(8,128)} %get-tuple-element.430, f32[6,512]{1,0:T(8,128)S(1)} %get-tuple-element.431, pred[512,2048]{1,0:T(8,128)(4,1)S(1)} %broadcast_compare_fusion.4), kind=kLoop, calls=%fused_computation.4.clone.1 | loop fusion | flops 25162752 | bytes 26238976 | tf_op jit(solution)/shard_map/while/body/eval_jaxpr/reduce_sum | solution.py:97
  113.6 11.6 fusion.130
  127.1 14.3 %fusion.128 = (f32[6,512]{1,0:T(8,128)S(1)}, f32[6,512,2048]{2,1,0:T(8,128)}) fusion(pred[512,2048]{1,0:T(8,128)(4,1)S(1)} %broadcast_compare_fusion.4, bf16[2048,6,64]{0,2,1:T(8,128)(2,1)} %get-tuple-element.469, bf16[4,512,6,64]{1,3,2,0:T(8,128)(2,1)} %get-tuple-element.468, s32[]{:T(128)S(6)} %copy.67), kind=kOutput, calls=%fused_computation.3.clone.1 | convolution fusion | flops 824177664 | bytes 28192772 | tf_op jit(solution)/shard_map/while/body/eval_jaxpr/qhd,khd->hqk/dot_general | solution.py:38
  141.3 12.1 %fusion.129 = f32[6,512]{1,0:T(8,128)S(1)} fusion(f32[6,512,2048]{2,1,0:T(8,128)} %get-tuple-element.430, f32[6,512]{1,0:T(8,128)S(1)} %get-tuple-element.431, pred[512,2048]{1,0:T(8,128)(4,1)S(1)} %broadcast_compare_fusion.4), kind=kLoop, calls=%fused_computation.4.clone.1 | loop fusion | flops 25162752 | bytes 26238976 | tf_op jit(solution)/shard_map/while/body/eval_jaxpr/reduce_sum | solution.py:97
  153.5 11.6 fusion.130
  166.9 14.3 %fusion.128 = (f32[6,512]{1,0:T(8,128)S(1)}, f32[6,512,2048]{2,1,0:T(8,128)}) fusion(pred[512,2048]{1,0:T(8,128)(4,1)S(1)} %broadcast_compare_fusion.4, bf16[2048,6,64]{0,2,1:T(8,128)(2,1)} %get-tuple-element.469, bf16[4,512,6,64]{1,3,2,0:T(8,128)(2,1)} %get-tuple-element.468, s32[]{:T(128)S(6)} %copy.67), kind=kOutput, calls=%fused_computation.3.clone.1 | convolution fusion | flops 824177664 | bytes 28192772 | tf_op jit(solution)/shard_map/while/body/eval_jaxpr/qhd,khd->hqk/dot_general | solution.py:38
  181.2 12.1 %fusion.129 = f32[6,512]{1,0:T(8,128)S(1)} fusion(f32[6,512,2048]{2,1,0:T(8,128)} %get-tuple-element.430, f32[6,512]{1,0:T(8,128)S(1)} %get-tuple-element.431, pred[512,2048]{1,0:T(8,128)(4,1)S(1)} %broadcast_compare_fusion.4), kind=kLoop, calls=%fused_computation.4.clone.1 | loop fusion | flops 25162752 | bytes 26238976 | tf_op jit(solution)/shard_map/while/body/eval_jaxpr/reduce_sum | solution.py:97
  193.3 11.6 fusion.130
  210.6 3.5 convolution_convert_fusion
  214.2 12.2 %reduce-scatter.5.cloned.1.call-done = bf16[1024,768]{1,0:T(8,128)(2,1)} async-done(((bf16[2048,768]{1,0:T(8,128)(2,1)}), bf16[1024,768]{1,0:T(8,128)(2,1)}) %reduce-scatter.5.cloned.1.call-update) | async-done | bytes 1572880 | tf_op jit(solution)/shard_map/reduce_scatter | solution.py:107
  234.2 41.9 %psum.63 = f32[3]{0:T(128)S(1)} all-reduce(f32[3]{0:T(128)S(1)} %compare_select_fusion.1), channel_id=1, replica_groups=mesh['dp'=16,'mp'=2] {'dp'}, use_global_device_ids=true, to_apply=%region_14.15 | all-reduce | flops 3 | bytes 24 | tf_op jit(solution)/shard_map/psum | solution.py:64
  282.4 13.7 %multiply_convert_fusion.1 = (bf16[2048,1536]{1,0:T(8,128)(2,1)}, f32[2048,1536]{1,0:T(8,128)}) fusion(f32[1536]{0:T(1024)S(1)} %copy-done.48, bf16[2048,768]{1,0:T(8,128)(2,1)} %all-gather.7.cloned.1.call-done, bf16[768,1536]{1,0:T(8,128)(2,1)S(1)} %copy-done), kind=kOutput, calls=%fused_computation.58 | convolution fusion | flops 4863295488 | bytes 24385536 | tf_op jit(solution)/shard_map/dot_general | solution.py:116
  296.1 19.5 %convert_reduce_fusion = (f32[1536]{0:T(1024)}, bf16[2048,1536]{1,0:T(8,128)(2,1)S(1)}) fusion(bf16[2048,768]{1,0:T(8,128)(2,1)} %all-gather.9.cloned.1.call-done, bf16[1536,768]{1,0:T(8,128)(2,1)} %param.27, f32[2048,1536]{1,0:T(8,128)} %get-tuple-element.318, f32[1536]{0:T(1024)S(1)} %copy-done.48), kind=kOutput, calls=%fused_computation.57 | convolution fusion | flops 4916771328 | bytes 24391680 | tf_op jit(solution)/shard_map/rd,fd->rf/dot_general | solution.py:132
  318.2 6.4 convolution_convert_fusion.1
  326.3 9.7 convolution_convert_fusion.2
  337.4 3.9 convert_reduce_fusion.2
  341.3 4.2 fusion.56
  346.4 5.6 fusion.77
  355.0 13.4 %all-gather.11.cloned.1.call-done = bf16[2048,768]{1,0:T(8,128)(2,1)} async-done(((bf16[1024,768]{1,0:T(8,128)(2,1)}), bf16[2048,768]{1,0:T(8,128)(2,1)}) %all-gather.11.cloned.1.call-update) | async-done | bytes 3145744 | tf_op jit(solution)/shard_map/all_gather | solution.py:149
  368.4 4.9 convolution_convert_fusion.3
  381.7 333.3 %while.28 = (s32[]{:T(128)}, f32[2048,6,64]{0,2,1:T(8,128)}, f32[2048,6,64]{0,2,1:T(8,128)}, bf16[4,512,6,64]{1,3,2,0:T(8,128)(2,1)}, bf16[4,512,6,64]{1,3,2,0:T...) while((s32[]{:T(128)}, f32[2048,6,64]{0,2,1:T(8,128)}, ...), condition=%wide.region_23.24_spmd.clone, body=%wide.region_21.23_spmd.clone.sunk | while | flops 4126077952 | bytes 212699312 | solution.py:188
  382.6 11.0 fusion.140
  393.7 12.8 %bitcast_add_fusion.5 = f32[2048,6,64]{0,2,1:T(8,128)} fusion(f32[2048,6,64]{0,2,1:T(8,128)} %get-tuple-element.487, f32[6,512,2048]{2,1,0:T(8,128)} %fusion.140, f32[6,512]{1,0:T(8,128)S(1)} %dynamic-slice_bitcast_fusion.2, pred[512,2048]{1,0:T(8,128)(4,1)S(1)} %broadcast_compare_fusion.5, pred[]{:T(512)S(6)} %compare.3, ...), kind=kOutput, calls=%fused_computation.23.clone.1 | convolution fusion | flops 832045056 | bytes 32911364 | tf_op jit(solution)/shard_map/while/body/eval_jaxpr/hqk,qhd->khd/dot_general | solution.py:163
  406.5 18.1 %multiply_reduce_fusion.3 = (f32[6,512]{1,0:T(8,128)S(1)}, f32[6,512,2048]{2,1,0:T(8,128)}) fusion(f32[6,512,2048]{2,1,0:T(8,128)} %fusion.140, f32[6,512]{1,0:T(8,128)S(1)} %dynamic-slice_bitcast_fusion.2, pred[512,2048]{1,0:T(8,128)(4,1)S(1)} %broadcast_compare_fusion.5, bf16[2048,6,64]{0,2,1:T(8,128)(2,1)} %get-tuple-element.508, ...), kind=kOutput, calls=%fused_computation.18.clone.1 | convolution fusion | flops 836760576 | bytes 53370884 | tf_op jit(solution)/shard_map/while/body/eval_jaxpr/qhd,khd->hqk/dot_general | solution.py:169
  424.6 21.3 %multiply_convert_fusion.3 = bf16[6,512,2048]{2,1,0:T(8,128)(2,1)} fusion(f32[6,512,2048]{2,1,0:T(8,128)} %get-tuple-element.443, f32[6,512,2048]{2,1,0:T(8,128)} %fusion.140, f32[6,512]{1,0:T(8,128)S(1)} %get-tuple-element.444, f32[6,512]{1,0:T(8,128)S(1)} %dynamic-slice_bitcast_fusion.2, pred[512,2048]{1,0:T(8,128)(4,1)S(1)} %broadcast_compare_fusion.5), kind=kLoop, calls=%fused_computation.17.clone.1 | loop fusion | flops 37748736 | bytes 63987712 | tf_op jit(solution)/shard_map/while/body/eval_jaxpr/convert_element_type | solution.py:173
  445.8 9.3 fusion.141
  455.1 8.7 bitcast_add_fusion.4
  464.5 11.0 fusion.140
  475.5 13.7 %bitcast_add_fusion.5 = f32[2048,6,64]{0,2,1:T(8,128)} fusion(f32[2048,6,64]{0,2,1:T(8,128)} %get-tuple-element.487, f32[6,512,2048]{2,1,0:T(8,128)} %fusion.140, f32[6,512]{1,0:T(8,128)S(1)} %dynamic-slice_bitcast_fusion.2, pred[512,2048]{1,0:T(8,128)(4,1)S(1)} %broadcast_compare_fusion.5, pred[]{:T(512)S(6)} %compare.3, ...), kind=kOutput, calls=%fused_computation.23.clone.1 | convolution fusion | flops 832045056 | bytes 32911364 | tf_op jit(solution)/shard_map/while/body/eval_jaxpr/hqk,qhd->khd/dot_general | solution.py:163
  489.2 18.1 %multiply_reduce_fusion.3 = (f32[6,512]{1,0:T(8,128)S(1)}, f32[6,512,2048]{2,1,0:T(8,128)}) fusion(f32[6,512,2048]{2,1,0:T(8,128)} %fusion.140, f32[6,512]{1,0:T(8,128)S(1)} %dynamic-slice_bitcast_fusion.2, pred[512,2048]{1,0:T(8,128)(4,1)S(1)} %broadcast_compare_fusion.5, bf16[2048,6,64]{0,2,1:T(8,128)(2,1)} %get-tuple-element.508, ...), kind=kOutput, calls=%fused_computation.18.clone.1 | convolution fusion | flops 836760576 | bytes 53370884 | tf_op jit(solution)/shard_map/while/body/eval_jaxpr/qhd,khd->hqk/dot_general | solution.py:169
  507.3 21.3 %multiply_convert_fusion.3 = bf16[6,512,2048]{2,1,0:T(8,128)(2,1)} fusion(f32[6,512,2048]{2,1,0:T(8,128)} %get-tuple-element.443, f32[6,512,2048]{2,1,0:T(8,128)} %fusion.140, f32[6,512]{1,0:T(8,128)S(1)} %get-tuple-element.444, f32[6,512]{1,0:T(8,128)S(1)} %dynamic-slice_bitcast_fusion.2, pred[512,2048]{1,0:T(8,128)(4,1)S(1)} %broadcast_compare_fusion.5), kind=kLoop, calls=%fused_computation.17.clone.1 | loop fusion | flops 37748736 | bytes 63987712 | tf_op jit(solution)/shard_map/while/body/eval_jaxpr/convert_element_type | solution.py:173
  528.6 9.3 fusion.141
  537.8 9.6 bitcast_add_fusion.4
  548.1 11.0 fusion.140
  559.1 13.7 %bitcast_add_fusion.5 = f32[2048,6,64]{0,2,1:T(8,128)} fusion(f32[2048,6,64]{0,2,1:T(8,128)} %get-tuple-element.487, f32[6,512,2048]{2,1,0:T(8,128)} %fusion.140, f32[6,512]{1,0:T(8,128)S(1)} %dynamic-slice_bitcast_fusion.2, pred[512,2048]{1,0:T(8,128)(4,1)S(1)} %broadcast_compare_fusion.5, pred[]{:T(512)S(6)} %compare.3, ...), kind=kOutput, calls=%fused_computation.23.clone.1 | convolution fusion | flops 832045056 | bytes 32911364 | tf_op jit(solution)/shard_map/while/body/eval_jaxpr/hqk,qhd->khd/dot_general | solution.py:163
  572.8 18.1 %multiply_reduce_fusion.3 = (f32[6,512]{1,0:T(8,128)S(1)}, f32[6,512,2048]{2,1,0:T(8,128)}) fusion(f32[6,512,2048]{2,1,0:T(8,128)} %fusion.140, f32[6,512]{1,0:T(8,128)S(1)} %dynamic-slice_bitcast_fusion.2, pred[512,2048]{1,0:T(8,128)(4,1)S(1)} %broadcast_compare_fusion.5, bf16[2048,6,64]{0,2,1:T(8,128)(2,1)} %get-tuple-element.508, ...), kind=kOutput, calls=%fused_computation.18.clone.1 | convolution fusion | flops 836760576 | bytes 53370884 | tf_op jit(solution)/shard_map/while/body/eval_jaxpr/qhd,khd->hqk/dot_general | solution.py:169
  590.9 21.3 %multiply_convert_fusion.3 = bf16[6,512,2048]{2,1,0:T(8,128)(2,1)} fusion(f32[6,512,2048]{2,1,0:T(8,128)} %get-tuple-element.443, f32[6,512,2048]{2,1,0:T(8,128)} %fusion.140, f32[6,512]{1,0:T(8,128)S(1)} %get-tuple-element.444, f32[6,512]{1,0:T(8,128)S(1)} %dynamic-slice_bitcast_fusion.2, pred[512,2048]{1,0:T(8,128)(4,1)S(1)} %broadcast_compare_fusion.5), kind=kLoop, calls=%fused_computation.17.clone.1 | loop fusion | flops 37748736 | bytes 63987712 | tf_op jit(solution)/shard_map/while/body/eval_jaxpr/convert_element_type | solution.py:173
  612.2 9.3 fusion.141
  621.4 9.6 bitcast_add_fusion.4
  631.7 11.0 fusion.140
  642.7 13.7 %bitcast_add_fusion.5 = f32[2048,6,64]{0,2,1:T(8,128)} fusion(f32[2048,6,64]{0,2,1:T(8,128)} %get-tuple-element.487, f32[6,512,2048]{2,1,0:T(8,128)} %fusion.140, f32[6,512]{1,0:T(8,128)S(1)} %dynamic-slice_bitcast_fusion.2, pred[512,2048]{1,0:T(8,128)(4,1)S(1)} %broadcast_compare_fusion.5, pred[]{:T(512)S(6)} %compare.3, ...), kind=kOutput, calls=%fused_computation.23.clone.1 | convolution fusion | flops 832045056 | bytes 32911364 | tf_op jit(solution)/shard_map/while/body/eval_jaxpr/hqk,qhd->khd/dot_general | solution.py:163
  656.4 18.1 %multiply_reduce_fusion.3 = (f32[6,512]{1,0:T(8,128)S(1)}, f32[6,512,2048]{2,1,0:T(8,128)}) fusion(f32[6,512,2048]{2,1,0:T(8,128)} %fusion.140, f32[6,512]{1,0:T(8,128)S(1)} %dynamic-slice_bitcast_fusion.2, pred[512,2048]{1,0:T(8,128)(4,1)S(1)} %broadcast_compare_fusion.5, bf16[2048,6,64]{0,2,1:T(8,128)(2,1)} %get-tuple-element.508, ...), kind=kOutput, calls=%fused_computation.18.clone.1 | convolution fusion | flops 836760576 | bytes 53370884 | tf_op jit(solution)/shard_map/while/body/eval_jaxpr/qhd,khd->hqk/dot_general | solution.py:169
  674.5 21.3 %multiply_convert_fusion.3 = bf16[6,512,2048]{2,1,0:T(8,128)(2,1)} fusion(f32[6,512,2048]{2,1,0:T(8,128)} %get-tuple-element.443, f32[6,512,2048]{2,1,0:T(8,128)} %fusion.140, f32[6,512]{1,0:T(8,128)S(1)} %get-tuple-element.444, f32[6,512]{1,0:T(8,128)S(1)} %dynamic-slice_bitcast_fusion.2, pred[512,2048]{1,0:T(8,128)(4,1)S(1)} %broadcast_compare_fusion.5), kind=kLoop, calls=%fused_computation.17.clone.1 | loop fusion | flops 37748736 | bytes 63987712 | tf_op jit(solution)/shard_map/while/body/eval_jaxpr/convert_element_type | solution.py:173
  695.8 9.3 fusion.141
  705.0 9.6 bitcast_add_fusion.4
  715.0 3.8 copy.52
  732.9 8.9 bitcast_convert_fusion
  741.9 9.8 fusion.81
  751.7 9.1 fusion.82
  764.5 5.8 fusion.66
  772.7 81.2 %all-reduce.1 = (f32[2,384]{1,0:T(2,128)}, f32[1536]{0:T(1024)}) all-reduce(f32[2,384]{1,0:T(2,128)S(1)} %pad_maximum_fusion.6, f32[1536]{0:T(1024)S(1)} %copy-done.38), channel_id=1, replica_groups=mesh['dp'=16,'mp'=2] {'dp'}, use_global_device_ids=true, to_apply=%region_38.39 | all-reduce | flops 2304 | bytes 18432 | tf_op jit(solution)/shard_map/psum | solution.py:234
  858.7 41.5 %all-reduce = (f32[2,768]{1,0:T(2,128)}, f32[4,768]{1,0:T(4,128)}) all-reduce(f32[2,768]{1,0:T(2,128)S(1)} %pad_maximum_fusion.5, f32[4,768]{1,0:T(4,128)S(1)} %pad_maximum_fusion.3), channel_id=1, replica_groups=mesh['dp'=16,'mp'=2] {'dp','mp'}, use_global_device_ids=true, to_apply=%region_29.30 | all-reduce | flops 4608 | bytes 36864 | tf_op jit(solution)/shard_map/psum | solution.py:220
  900.1 4.1 add_add_fusion.2
  904.2 267.0 %all-reduce.5.cloned.1.call-done = (f32[3,768,384]{1,2,0:T(8,128)}, f32[384,768]{1,0:T(8,128)}, f32[768,1536]{1,0:T(8,128)}, f32[1536,768]{1,0:T(8,128)}) async-done(((f32[3,768,384]{1,2,0:T(8,128)}, f32[384,768]{1,0:T(8,128)}, f32[768,1536]{1,0:T(8,128)}, f32[1536,768]{1,0:T(8,128)}), (f32[3,768,384]{1,2,0:T(8,128)}, f32[384,768]{1,0:T(8,128)}, f32[768,1536]{1,0:T(8,128)}, ...) | async-done | bytes 14155792 | tf_op jit(solution)/shard_map/psum | solution.py:234
  1171.3 5.2 copy.57
  1177.5 5.5 copy.92
  (237 shorter events, 87.9 us)
Async XLA Ops:
  7.2 275.3 %copy-start = (bf16[768,1536]{1,0:T(8,128)(2,1)S(1)}, bf16[768,1536]{1,0:T(8,128)(2,1)}, u32[]{:S(2)}) copy-start(bf16[768,1536]{1,0:T(8,128)(2,1)} %param.25) | copy-start | bytes 7077892
  7.2 4.6 copy-start.39
  7.2 5.2 copy-start.37
  7.2 22.6 %all-gather.5.cloned.1.call-start = ((), (), s32[]{:S(2)}) async-start(), calls=%async_computation.4 | async-start | bytes 4718592 | tf_op jit(solution)/shard_map/all_gather | solution.py:78
  7.3 5.8 copy-start.3
  9.1 3.9 copy-start.22
  9.1 5.8 copy-start.41
  9.1 6.3 copy-start.40
  11.8 1.3 copy-start.27
  14.8 211.6 %reduce-scatter.5.cloned.1.call-start = ((), (), s32[]{:S(2)}) async-start(), calls=%async_computation.5 | async-start | bytes 4718592 | tf_op jit(solution)/shard_map/reduce_scatter | solution.py:107
  61.6 12.1 %copy-start.7 = (bf16[2048,6,64]{0,2,1:T(8,128)(2,1)S(1)}, bf16[2048,6,64]{0,2,1:T(8,128)(2,1)}, u32[]{:S(2)}) copy-start(bf16[2048,6,64]{0,2,1:T(8,128)(2,1)} %get-tuple-element.470) | copy-start | bytes 4718596 | tf_op jit(solution)/shard_map/while
  61.6 12.1 %copy-start.13 = (bf16[4,512,6,64]{1,3,2,0:T(8,128)(2,1)S(1)}, bf16[4,512,6,64]{1,3,2,0:T(8,128)(2,1)}, u32[]{:S(2)}) copy-start(bf16[4,512,6,64]{1,3,2,0:T(8,128)(2,1)} %get-tuple-element.455) | copy-start | bytes 4718596 | tf_op jit(solution)/shard_map/while
  85.4 1.1 copy-start.14
  101.5 12.1 %copy-start.7 = (bf16[2048,6,64]{0,2,1:T(8,128)(2,1)S(1)}, bf16[2048,6,64]{0,2,1:T(8,128)(2,1)}, u32[]{:S(2)}) copy-start(bf16[2048,6,64]{0,2,1:T(8,128)(2,1)} %get-tuple-element.470) | copy-start | bytes 4718596 | tf_op jit(solution)/shard_map/while
  101.5 12.1 %copy-start.13 = (bf16[4,512,6,64]{1,3,2,0:T(8,128)(2,1)S(1)}, bf16[4,512,6,64]{1,3,2,0:T(8,128)(2,1)}, u32[]{:S(2)}) copy-start(bf16[4,512,6,64]{1,3,2,0:T(8,128)(2,1)} %get-tuple-element.455) | copy-start | bytes 4718596 | tf_op jit(solution)/shard_map/while
  125.2 1.1 copy-start.14
  141.3 12.1 %copy-start.7 = (bf16[2048,6,64]{0,2,1:T(8,128)(2,1)S(1)}, bf16[2048,6,64]{0,2,1:T(8,128)(2,1)}, u32[]{:S(2)}) copy-start(bf16[2048,6,64]{0,2,1:T(8,128)(2,1)} %get-tuple-element.470) | copy-start | bytes 4718596 | tf_op jit(solution)/shard_map/while
  141.3 12.1 %copy-start.13 = (bf16[4,512,6,64]{1,3,2,0:T(8,128)(2,1)S(1)}, bf16[4,512,6,64]{1,3,2,0:T(8,128)(2,1)}, u32[]{:S(2)}) copy-start(bf16[4,512,6,64]{1,3,2,0:T(8,128)(2,1)} %get-tuple-element.455) | copy-start | bytes 4718596 | tf_op jit(solution)/shard_map/while
  165.1 1.1 copy-start.14
  181.2 12.1 %copy-start.7 = (bf16[2048,6,64]{0,2,1:T(8,128)(2,1)S(1)}, bf16[2048,6,64]{0,2,1:T(8,128)(2,1)}, u32[]{:S(2)}) copy-start(bf16[2048,6,64]{0,2,1:T(8,128)(2,1)} %get-tuple-element.470) | copy-start | bytes 4718596 | tf_op jit(solution)/shard_map/while
  181.2 12.1 %copy-start.13 = (bf16[4,512,6,64]{1,3,2,0:T(8,128)(2,1)S(1)}, bf16[4,512,6,64]{1,3,2,0:T(8,128)(2,1)}, u32[]{:S(2)}) copy-start(bf16[4,512,6,64]{1,3,2,0:T(8,128)(2,1)} %get-tuple-element.455) | copy-start | bytes 4718596 | tf_op jit(solution)/shard_map/while
  205.0 1.1 copy-start.14
  206.3 4.3 copy-start.47
  209.4 1.2 copy-start.15
  214.1 12.3 %copy-start.21 = (f32[768]{0:T(1024)S(1)}, f32[768]{0:T(1024)}, u32[]{:S(2)}) copy-start(f32[768]{0:T(1024)} %get-tuple-element.249) | copy-start | bytes 9220
  214.2 68.3 %all-gather.7.cloned.1.call-start = ((), (), s32[]{:S(2)}) async-start(), calls=%async_computation.6 | async-start | bytes 4718592 | tf_op jit(solution)/shard_map/all_gather | solution.py:115
  226.4 2.6 copy-start.4
  226.4 2.8 copy-start.8
  226.4 3.7 copy-start.26
  226.4 3.7 copy-start.34
  230.1 2.8 copy-start.42
  232.2 50.3 %copy-start.48 = (f32[1536]{0:T(1024)S(1)}, f32[1536]{0:T(1024)}, u32[]{:S(2)}) copy-start(f32[1536]{0:T(1024)} %param.26) | copy-start | bytes 18436
  232.2 64.0 %all-gather.9.cloned.1.call-start = ((), (), s32[]{:S(2)}) async-start(), calls=%async_computation.8 | async-start | bytes 4718592 | tf_op jit(solution)/shard_map/all_gather | solution.py:128
  282.4 54.2 %reduce-scatter.9.cloned.1.call-start = ((), (), s32[]{:S(2)}) async-start(), calls=%async_computation.9 | async-start | bytes 4718592 | tf_op jit(solution)/shard_map/reduce_scatter | solution.py:139
  315.6 2.6 copy-start.49
  324.6 1.7 copy-start.46
  324.7 21.7 %reduce-scatter.7.cloned.1.call-start = ((), (), s32[]{:S(2)}) async-start(), calls=%async_computation.7 | async-start | bytes 4718592 | tf_op jit(solution)/shard_map/reduce_scatter | solution.py:120
  335.9 1.4 copy-start.5
  336.0 32.4 %all-gather.11.cloned.1.call-start = ((), (), s32[]{:S(2)}) async-start(), calls=%async_computation.10 | async-start | bytes 4718592 | tf_op jit(solution)/shard_map/all_gather | solution.py:149
  337.4 3.9 copy-start.12
  341.2 5.1 copy-start.31
  351.9 1.7 copy-start.9
  354.9 499.0 %reduce-scatter.11.cloned.1.call-start = ((), (), s32[]{:S(2)}) async-start(), calls=%async_computation.11 | async-start | bytes 4718592 | tf_op jit(solution)/shard_map/reduce_scatter | solution.py:210
  377.3 4.4 copy-start.2
  721.6 5.0 copy-start.10
  741.8 429.4 %all-reduce.5.cloned.1.call-start = ((), (), s32[]{:S(2)}) async-start(), calls=%async_computation.12 | async-start | bytes 28311552 | tf_op jit(solution)/shard_map/psum | solution.py:234
  741.9 9.8 copy-start.44
  751.7 9.1 copy-start.16
  751.7 9.1 copy-start.45
  760.7 2.4 copy-start.17
  760.8 2.4 copy-start.18
  760.8 2.4 copy-start.19
  760.8 3.7 copy-start.43
  770.3 2.5 copy-start.38
  770.3 83.7 %copy-start.6 = (bf16[1024,768]{1,0:T(8,128)(2,1)S(1)}, bf16[1024,768]{1,0:T(8,128)(2,1)}, u32[]{:S(2)}) copy-start(bf16[1024,768]{1,0:T(8,128)(2,1)} %param.16) | copy-start | bytes 4718596
  770.3 83.7 %copy-start.23 = (f32[1024]{0:T(1024)S(1)}, f32[1024]{0:T(1024)}, u32[]{:S(2)}) copy-start(f32[1024]{0:T(1024)} %copy-done.22) | copy-start | bytes 12292
  770.3 83.6 %copy-start.25 = (f32[768]{0:T(1024)S(1)}, f32[768]{0:T(1024)}, u32[]{:S(2)}) copy-start(f32[768]{0:T(1024)} %copy-done.24) | copy-start | bytes 9220
  770.3 86.3 %copy-start.30 = (f32[1024]{0:T(1024)S(1)}, f32[1024]{0:T(1024)}, u32[]{:S(2)}) copy-start(f32[1024]{0:T(1024)} %copy-done.29) | copy-start | bytes 12292
  770.3 86.3 %copy-start.28 = (f32[1024]{0:T(1024)S(1)}, f32[1024]{0:T(1024)}, u32[]{:S(2)}) copy-start(f32[1024]{0:T(1024)} %copy-done.27) | copy-start | bytes 12292
  854.0 2.7 copy-start.11
  1171.3 5.3 copy-start.20
  1176.5 6.5 slice-start
  1177.5 5.5 slice-start.1
  1177.5 7.7 copy-start.1
  (6 other events, 4.0 us)
Sparse Core Ops, SparseCore 0:
  15.0 14.8 all-gather.4
  214.3 12.0 reduce-scatter.4
  232.3 13.3 all-gather.6
  282.5 7.9 all-gather.8
  324.8 6.7 reduce-scatter.8
  336.1 10.2 reduce-scatter.6
  355.1 13.2 all-gather.10
  742.0 12.0 reduce-scatter.10
  770.5 400.7 all-reduce.4
where the time goes:
time: 1200 us; the launch traced here: 1190 us
  matrix products  448 us (37%)
  waiting for transfers between devices  308 us (26%)
  other arithmetic  188 us (16%)
  blocking collectives  165 us (14%)
  local copies, waits for them, and re-layouts  65.3 us (5%)
  between operations  15.9 us (1%)
    psum x1, waiting for transfers between devices, local(): lax.psum((grad_qkv, grad_qv_bias, grad_out, grad_fc1, grad_bfc1, grad_fc2...  267 us
    dot_general x8, matrix products, score_block(): jnp.einsum('qhd,khd->hqk', query_block, keys_all, preferred_element_type=...  101 us
    convert_element_type x4, other arithmetic, backward_block(): grad_scores = grad_scores.astype(jnp.bfloat16)  85.1 us
    psum x1, blocking collectives, local(): lax.psum((grad_qkv, grad_qv_bias, grad_out, grad_fc1, grad_bfc1, grad_fc2...  81.2 us
    dot_general x4, matrix products, backward_block(): jnp.einsum('qhd,khd->hqk', grad_block, values_all, preferred_element_type...  72.3 us
    dot_general x4, matrix products, backward_block(): jnp.einsum('hqk,qhd->khd', probs.astype(jnp.bfloat16), grad_block, prefer...  53.8 us
    reduce_sum x4, other arithmetic, forward_block(): total = jnp.sum(exponent, axis=-1, keepdims=True)  48.4 us
    dot_general x4, matrix products, forward_block(): jnp.einsum('hqk,khd->qhd', weights, values_all, preferred_element_type=jn...  46.6 us
  transfers between devices with their start and end apart: 9, of which 5 were waited for; matrix products, arithmetic and copies ran while one was open for 6% of the time, Pallas kernels for 0%

commit v1 on v0

--- a/solution.py
+++ b/solution.py
@@ -6,6 +6,11 @@
 HEAD_DIM = 64
 GROUPS = 3
 LEN_NORM = 64
+
+
+def cut_the_units(mat, mesh_dim, net_axis):
+    found_now = lax.psum(lax.psum(mat, axis_name=mesh_dim), axis_name=net_axis)
+    return found_now
 
 
 def layer_norm(values, gain_vec, shift_vec):
@@ -217,7 +222,7 @@
     ).astype(jnp.float32)
     grad_input, grad_gain_one, grad_shift_one = norm_pull(grad_norm_one)
     grad_input = grad_input + grad_hidden
-    gain_grads, shift_grads = lax.psum(
+    gain_grads, shift_grads = cut_the_units(
         (
             jnp.stack([grad_gain_one, grad_gain_two]),
             jnp.stack(
@@ -229,7 +234,8 @@
                 ]
             ),
         ),
-        ("dp", "mp"),
+        "mp",
+        "dp",
     )
     grad_qkv, grad_qv_bias, grad_out, grad_fc1, grad_bfc1, grad_fc2 = lax.psum(
         (grad_qkv, grad_qv_bias, grad_out, grad_fc1, grad_bfc1, grad_fc2), "dp"

time: 1200 us -> 1200 us (level)
  blocking collectives: 165 us -> 127 us
  waiting for transfers between devices: 308 us -> 344 us
    psum x2, blocking collectives: 123 us -> 85.2 us  [cut_the_units(): found_now = lax.psum(lax.psum(mat, axis_name=mesh_dim), axis_name=net_axis)]
    psum x1, waiting for transfers between devices: 267 us -> 303 us  [local(): lax.psum((grad_qkv, grad_qv_bias, grad_out, grad_fc1, grad_bfc1, grad_fc2...]
where the time goes in v1:
time: 1200 us; the launch traced here: 1190 us
  matrix products  448 us (37%)
  waiting for transfers between devices  344 us (29%)
  other arithmetic  188 us (16%)
  blocking collectives  127 us (11%)
  local copies, waits for them, and re-layouts  65.3 us (5%)
  between operations  16 us (1%)
    psum x1, waiting for transfers between devices, local(): lax.psum((grad_qkv, grad_qv_bias, grad_out, grad_fc1, grad_bfc1, grad_fc2...  303 us
    dot_general x8, matrix products, score_block(): jnp.einsum('qhd,khd->hqk', query_block, keys_all, preferred_element_type=...  101 us
    psum x2, blocking collectives, cut_the_units(): found_now = lax.psum(lax.psum(mat, axis_name=mesh_dim), axis_name=net_axis)  85.2 us
    convert_element_type x4, other arithmetic, backward_block(): grad_scores = grad_scores.astype(jnp.bfloat16)  85.1 us
    dot_general x4, matrix products, backward_block(): jnp.einsum('qhd,khd->hqk', grad_block, values_all, preferred_element_type...  72.3 us
    dot_general x4, matrix products, backward_block(): jnp.einsum('hqk,qhd->khd', probs.astype(jnp.bfloat16), grad_block, prefer...  53.8 us
    reduce_sum x4, other arithmetic, forward_block(): total = jnp.sum(exponent, axis=-1, keepdims=True)  48.4 us
    dot_general x4, matrix products, forward_block(): jnp.einsum('hqk,khd->qhd', weights, values_all, preferred_element_type=jn...  46.6 us
  transfers between devices with their start and end apart: 9, of which 5 were waited for; matrix products, arithmetic and copies ran while one was open for 6% of the time, Pallas kernels for 0%

profile of v1, /device:TPU:0, one launch (start us, length us, event | category | flops | bytes accessed | tf_op | source)
XLA Modules:
  0.0 1190.8 jit_solution(8026270459712380475)
XLA Ops:
  15.6 14.2 %all-gather.5.cloned.1.call-done = bf16[2048,768]{1,0:T(8,128)(2,1)} async-done(((bf16[1024,768]{1,0:T(8,128)(2,1)}), bf16[2048,768]{1,0:T(8,128)(2,1)}) %all-gather.5.cloned.1.call-update) | async-done | bytes 3145744 | tf_op jit(solution)/shard_map/all_gather | solution.py:83
  29.8 6.3 fusion.45
  38.5 4.0 reshape_squeeze.3
  46.7 159.6 %while.27 = (s32[]{:T(128)}, bf16[4,512,6,64]{1,3,2,0:T(8,128)(2,1)}, f32[4,6,512]{2,1,0:T(8,128)S(1)}, s32[4,512]{1,0:T(4,128)S(1)}, s32[2048]{0:T(1024)S(1)}, ...) while((s32[]{:T(128)}, ...), condition=%wide.region_7.8_spmd, body=%wide.region_4.7_spmd.sunk | while | flops 1687155712 | bytes 103024832 | solution.py:109
  47.3 14.3 %fusion.128 = (f32[6,512]{1,0:T(8,128)S(1)}, f32[6,512,2048]{2,1,0:T(8,128)}) fusion(pred[512,2048]{1,0:T(8,128)(4,1)S(1)} %broadcast_compare_fusion.4, bf16[2048,6,64]{0,2,1:T(8,128)(2,1)} %get-tuple-element.471, bf16[4,512,6,64]{1,3,2,0:T(8,128)(2,1)} %get-tuple-element.470, s32[]{:T(128)S(6)} %copy.67), kind=kOutput, calls=%fused_computation.3.clone.1 | convolution fusion | flops 824177664 | bytes 28192772 | tf_op jit(solution)/shard_map/while/body/eval_jaxpr/qhd,khd->hqk/dot_general | solution.py:43
  61.6 12.1 %fusion.129 = f32[6,512]{1,0:T(8,128)S(1)} fusion(f32[6,512,2048]{2,1,0:T(8,128)} %get-tuple-element.432, f32[6,512]{1,0:T(8,128)S(1)} %get-tuple-element.433, pred[512,2048]{1,0:T(8,128)(4,1)S(1)} %broadcast_compare_fusion.4), kind=kLoop, calls=%fused_computation.4.clone.1 | loop fusion | flops 25162752 | bytes 26238976 | tf_op jit(solution)/shard_map/while/body/eval_jaxpr/reduce_sum | solution.py:102
  73.7 11.6 fusion.130
  87.2 14.3 %fusion.128 = (f32[6,512]{1,0:T(8,128)S(1)}, f32[6,512,2048]{2,1,0:T(8,128)}) fusion(pred[512,2048]{1,0:T(8,128)(4,1)S(1)} %broadcast_compare_fusion.4, bf16[2048,6,64]{0,2,1:T(8,128)(2,1)} %get-tuple-element.471, bf16[4,512,6,64]{1,3,2,0:T(8,128)(2,1)} %get-tuple-element.470, s32[]{:T(128)S(6)} %copy.67), kind=kOutput, calls=%fused_computation.3.clone.1 | convolution fusion | flops 824177664 | bytes 28192772 | tf_op jit(solution)/shard_map/while/body/eval_jaxpr/qhd,khd->hqk/dot_general | solution.py:43
  101.5 12.1 %fusion.129 = f32[6,512]{1,0:T(8,128)S(1)} fusion(f32[6,512,2048]{2,1,0:T(8,128)} %get-tuple-element.432, f32[6,512]{1,0:T(8,128)S(1)} %get-tuple-element.433, pred[512,2048]{1,0:T(8,128)(4,1)S(1)} %broadcast_compare_fusion.4), kind=kLoop, calls=%fused_computation.4.clone.1 | loop fusion | flops 25162752 | bytes 26238976 | tf_op jit(solution)/shard_map/while/body/eval_jaxpr/reduce_sum | solution.py:102
  113.6 11.6 fusion.130
  127.1 14.3 %fusion.128 = (f32[6,512]{1,0:T(8,128)S(1)}, f32[6,512,2048]{2,1,0:T(8,128)}) fusion(pred[512,2048]{1,0:T(8,128)(4,1)S(1)} %broadcast_compare_fusion.4, bf16[2048,6,64]{0,2,1:T(8,128)(2,1)} %get-tuple-element.471, bf16[4,512,6,64]{1,3,2,0:T(8,128)(2,1)} %get-tuple-element.470, s32[]{:T(128)S(6)} %copy.67), kind=kOutput, calls=%fused_computation.3.clone.1 | convolution fusion | flops 824177664 | bytes 28192772 | tf_op jit(solution)/shard_map/while/body/eval_jaxpr/qhd,khd->hqk/dot_general | solution.py:43
  141.3 12.1 %fusion.129 = f32[6,512]{1,0:T(8,128)S(1)} fusion(f32[6,512,2048]{2,1,0:T(8,128)} %get-tuple-element.432, f32[6,512]{1,0:T(8,128)S(1)} %get-tuple-element.433, pred[512,2048]{1,0:T(8,128)(4,1)S(1)} %broadcast_compare_fusion.4), kind=kLoop, calls=%fused_computation.4.clone.1 | loop fusion | flops 25162752 | bytes 26238976 | tf_op jit(solution)/shard_map/while/body/eval_jaxpr/reduce_sum | solution.py:102
  153.5 11.6 fusion.130
  166.9 14.3 %fusion.128 = (f32[6,512]{1,0:T(8,128)S(1)}, f32[6,512,2048]{2,1,0:T(8,128)}) fusion(pred[512,2048]{1,0:T(8,128)(4,1)S(1)} %broadcast_compare_fusion.4, bf16[2048,6,64]{0,2,1:T(8,128)(2,1)} %get-tuple-element.471, bf16[4,512,6,64]{1,3,2,0:T(8,128)(2,1)} %get-tuple-element.470, s32[]{:T(128)S(6)} %copy.67), kind=kOutput, calls=%fused_computation.3.clone.1 | convolution fusion | flops 824177664 | bytes 28192772 | tf_op jit(solution)/shard_map/while/body/eval_jaxpr/qhd,khd->hqk/dot_general | solution.py:43
  181.2 12.1 %fusion.129 = f32[6,512]{1,0:T(8,128)S(1)} fusion(f32[6,512,2048]{2,1,0:T(8,128)} %get-tuple-element.432, f32[6,512]{1,0:T(8,128)S(1)} %get-tuple-element.433, pred[512,2048]{1,0:T(8,128)(4,1)S(1)} %broadcast_compare_fusion.4), kind=kLoop, calls=%fused_computation.4.clone.1 | loop fusion | flops 25162752 | bytes 26238976 | tf_op jit(solution)/shard_map/while/body/eval_jaxpr/reduce_sum | solution.py:102
  193.3 11.6 fusion.130
  210.6 3.5 convolution_convert_fusion
  214.2 12.2 %reduce-scatter.5.cloned.1.call-done = bf16[1024,768]{1,0:T(8,128)(2,1)} async-done(((bf16[2048,768]{1,0:T(8,128)(2,1)}), bf16[1024,768]{1,0:T(8,128)(2,1)}) %reduce-scatter.5.cloned.1.call-update) | async-done | bytes 1572880 | tf_op jit(solution)/shard_map/reduce_scatter | solution.py:112
  234.2 41.9 %psum.77 = f32[3]{0:T(128)S(1)} all-reduce(f32[3]{0:T(128)S(1)} %compare_select_fusion.1), channel_id=1, replica_groups=mesh['dp'=16,'mp'=2] {'dp'}, use_global_device_ids=true, to_apply=%region_14.15 | all-reduce | flops 3 | bytes 24 | tf_op jit(solution)/shard_map/psum | solution.py:69
  282.4 13.7 %multiply_convert_fusion.1 = (bf16[2048,1536]{1,0:T(8,128)(2,1)}, f32[2048,1536]{1,0:T(8,128)}) fusion(f32[1536]{0:T(1024)S(1)} %copy-done.48, bf16[2048,768]{1,0:T(8,128)(2,1)} %all-gather.7.cloned.1.call-done, bf16[768,1536]{1,0:T(8,128)(2,1)S(1)} %copy-done), kind=kOutput, calls=%fused_computation.58 | convolution fusion | flops 4863295488 | bytes 24385536 | tf_op jit(solution)/shard_map/dot_general | solution.py:121
  296.1 19.5 %convert_reduce_fusion = (f32[1536]{0:T(1024)}, bf16[2048,1536]{1,0:T(8,128)(2,1)S(1)}) fusion(bf16[2048,768]{1,0:T(8,128)(2,1)} %all-gather.9.cloned.1.call-done, bf16[1536,768]{1,0:T(8,128)(2,1)} %param.27, f32[2048,1536]{1,0:T(8,128)} %get-tuple-element.320, f32[1536]{0:T(1024)S(1)} %copy-done.48), kind=kOutput, calls=%fused_computation.57 | convolution fusion | flops 4916771328 | bytes 24391680 | tf_op jit(solution)/shard_map/rd,fd->rf/dot_general | solution.py:137
  318.2 6.4 convolution_convert_fusion.1
  326.3 9.7 convolution_convert_fusion.2
  337.4 3.9 convert_reduce_fusion.2
  341.3 4.2 fusion.56
  346.4 5.6 fusion.77
  355.0 13.4 %all-gather.11.cloned.1.call-done = bf16[2048,768]{1,0:T(8,128)(2,1)} async-done(((bf16[1024,768]{1,0:T(8,128)(2,1)}), bf16[2048,768]{1,0:T(8,128)(2,1)}) %all-gather.11.cloned.1.call-update) | async-done | bytes 3145744 | tf_op jit(solution)/shard_map/all_gather | solution.py:154
  368.4 4.9 convolution_convert_fusion.3
  381.7 333.3 %while.28 = (s32[]{:T(128)}, f32[2048,6,64]{0,2,1:T(8,128)}, f32[2048,6,64]{0,2,1:T(8,128)}, bf16[4,512,6,64]{1,3,2,0:T(8,128)(2,1)}, bf16[4,512,6,64]{1,3,2,0:T...) while((s32[]{:T(128)}, f32[2048,6,64]{0,2,1:T(8,128)}, ...), condition=%wide.region_23.24_spmd.clone, body=%wide.region_21.23_spmd.clone.sunk | while | flops 4126077952 | bytes 212699312 | solution.py:193
  382.6 11.0 fusion.140
  393.7 12.8 %bitcast_add_fusion.5 = f32[2048,6,64]{0,2,1:T(8,128)} fusion(f32[2048,6,64]{0,2,1:T(8,128)} %get-tuple-element.489, f32[6,512,2048]{2,1,0:T(8,128)} %fusion.140, f32[6,512]{1,0:T(8,128)S(1)} %dynamic-slice_bitcast_fusion.2, pred[512,2048]{1,0:T(8,128)(4,1)S(1)} %broadcast_compare_fusion.5, pred[]{:T(512)S(6)} %compare.3, ...), kind=kOutput, calls=%fused_computation.23.clone.1 | convolution fusion | flops 832045056 | bytes 32911364 | tf_op jit(solution)/shard_map/while/body/eval_jaxpr/hqk,qhd->khd/dot_general | solution.py:168
  406.5 18.1 %multiply_reduce_fusion.3 = (f32[6,512]{1,0:T(8,128)S(1)}, f32[6,512,2048]{2,1,0:T(8,128)}) fusion(f32[6,512,2048]{2,1,0:T(8,128)} %fusion.140, f32[6,512]{1,0:T(8,128)S(1)} %dynamic-slice_bitcast_fusion.2, pred[512,2048]{1,0:T(8,128)(4,1)S(1)} %broadcast_compare_fusion.5, bf16[2048,6,64]{0,2,1:T(8,128)(2,1)} %get-tuple-element.510, ...), kind=kOutput, calls=%fused_computation.18.clone.1 | convolution fusion | flops 836760576 | bytes 53370884 | tf_op jit(solution)/shard_map/while/body/eval_jaxpr/qhd,khd->hqk/dot_general | solution.py:174
  424.6 21.3 %multiply_convert_fusion.3 = bf16[6,512,2048]{2,1,0:T(8,128)(2,1)} fusion(f32[6,512,2048]{2,1,0:T(8,128)} %get-tuple-element.445, f32[6,512,2048]{2,1,0:T(8,128)} %fusion.140, f32[6,512]{1,0:T(8,128)S(1)} %get-tuple-element.446, f32[6,512]{1,0:T(8,128)S(1)} %dynamic-slice_bitcast_fusion.2, pred[512,2048]{1,0:T(8,128)(4,1)S(1)} %broadcast_compare_fusion.5), kind=kLoop, calls=%fused_computation.17.clone.1 | loop fusion | flops 37748736 | bytes 63987712 | tf_op jit(solution)/shard_map/while/body/eval_jaxpr/convert_element_type | solution.py:178
  445.8 9.3 fusion.141
  455.1 8.7 bitcast_add_fusion.4
  464.5 11.0 fusion.140
  475.5 13.7 %bitcast_add_fusion.5 = f32[2048,6,64]{0,2,1:T(8,128)} fusion(f32[2048,6,64]{0,2,1:T(8,128)} %get-tuple-element.489, f32[6,512,2048]{2,1,0:T(8,128)} %fusion.140, f32[6,512]{1,0:T(8,128)S(1)} %dynamic-slice_bitcast_fusion.2, pred[512,2048]{1,0:T(8,128)(4,1)S(1)} %broadcast_compare_fusion.5, pred[]{:T(512)S(6)} %compare.3, ...), kind=kOutput, calls=%fused_computation.23.clone.1 | convolution fusion | flops 832045056 | bytes 32911364 | tf_op jit(solution)/shard_map/while/body/eval_jaxpr/hqk,qhd->khd/dot_general | solution.py:168
  489.2 18.1 %multiply_reduce_fusion.3 = (f32[6,512]{1,0:T(8,128)S(1)}, f32[6,512,2048]{2,1,0:T(8,128)}) fusion(f32[6,512,2048]{2,1,0:T(8,128)} %fusion.140, f32[6,512]{1,0:T(8,128)S(1)} %dynamic-slice_bitcast_fusion.2, pred[512,2048]{1,0:T(8,128)(4,1)S(1)} %broadcast_compare_fusion.5, bf16[2048,6,64]{0,2,1:T(8,128)(2,1)} %get-tuple-element.510, ...), kind=kOutput, calls=%fused_computation.18.clone.1 | convolution fusion | flops 836760576 | bytes 53370884 | tf_op jit(solution)/shard_map/while/body/eval_jaxpr/qhd,khd->hqk/dot_general | solution.py:174
  507.3 21.3 %multiply_convert_fusion.3 = bf16[6,512,2048]{2,1,0:T(8,128)(2,1)} fusion(f32[6,512,2048]{2,1,0:T(8,128)} %get-tuple-element.445, f32[6,512,2048]{2,1,0:T(8,128)} %fusion.140, f32[6,512]{1,0:T(8,128)S(1)} %get-tuple-element.446, f32[6,512]{1,0:T(8,128)S(1)} %dynamic-slice_bitcast_fusion.2, pred[512,2048]{1,0:T(8,128)(4,1)S(1)} %broadcast_compare_fusion.5), kind=kLoop, calls=%fused_computation.17.clone.1 | loop fusion | flops 37748736 | bytes 63987712 | tf_op jit(solution)/shard_map/while/body/eval_jaxpr/convert_element_type | solution.py:178
  528.6 9.3 fusion.141
  537.8 9.6 bitcast_add_fusion.4
  548.1 11.0 fusion.140
  559.1 13.7 %bitcast_add_fusion.5 = f32[2048,6,64]{0,2,1:T(8,128)} fusion(f32[2048,6,64]{0,2,1:T(8,128)} %get-tuple-element.489, f32[6,512,2048]{2,1,0:T(8,128)} %fusion.140, f32[6,512]{1,0:T(8,128)S(1)} %dynamic-slice_bitcast_fusion.2, pred[512,2048]{1,0:T(8,128)(4,1)S(1)} %broadcast_compare_fusion.5, pred[]{:T(512)S(6)} %compare.3, ...), kind=kOutput, calls=%fused_computation.23.clone.1 | convolution fusion | flops 832045056 | bytes 32911364 | tf_op jit(solution)/shard_map/while/body/eval_jaxpr/hqk,qhd->khd/dot_general | solution.py:168
  572.8 18.1 %multiply_reduce_fusion.3 = (f32[6,512]{1,0:T(8,128)S(1)}, f32[6,512,2048]{2,1,0:T(8,128)}) fusion(f32[6,512,2048]{2,1,0:T(8,128)} %fusion.140, f32[6,512]{1,0:T(8,128)S(1)} %dynamic-slice_bitcast_fusion.2, pred[512,2048]{1,0:T(8,128)(4,1)S(1)} %broadcast_compare_fusion.5, bf16[2048,6,64]{0,2,1:T(8,128)(2,1)} %get-tuple-element.510, ...), kind=kOutput, calls=%fused_computation.18.clone.1 | convolution fusion | flops 836760576 | bytes 53370884 | tf_op jit(solution)/shard_map/while/body/eval_jaxpr/qhd,khd->hqk/dot_general | solution.py:174
  590.9 21.3 %multiply_convert_fusion.3 = bf16[6,512,2048]{2,1,0:T(8,128)(2,1)} fusion(f32[6,512,2048]{2,1,0:T(8,128)} %get-tuple-element.445, f32[6,512,2048]{2,1,0:T(8,128)} %fusion.140, f32[6,512]{1,0:T(8,128)S(1)} %get-tuple-element.446, f32[6,512]{1,0:T(8,128)S(1)} %dynamic-slice_bitcast_fusion.2, pred[512,2048]{1,0:T(8,128)(4,1)S(1)} %broadcast_compare_fusion.5), kind=kLoop, calls=%fused_computation.17.clone.1 | loop fusion | flops 37748736 | bytes 63987712 | tf_op jit(solution)/shard_map/while/body/eval_jaxpr/convert_element_type | solution.py:178
  612.2 9.3 fusion.141
  621.4 9.6 bitcast_add_fusion.4
  631.7 11.0 fusion.140
  642.7 13.7 %bitcast_add_fusion.5 = f32[2048,6,64]{0,2,1:T(8,128)} fusion(f32[2048,6,64]{0,2,1:T(8,128)} %get-tuple-element.489, f32[6,512,2048]{2,1,0:T(8,128)} %fusion.140, f32[6,512]{1,0:T(8,128)S(1)} %dynamic-slice_bitcast_fusion.2, pred[512,2048]{1,0:T(8,128)(4,1)S(1)} %broadcast_compare_fusion.5, pred[]{:T(512)S(6)} %compare.3, ...), kind=kOutput, calls=%fused_computation.23.clone.1 | convolution fusion | flops 832045056 | bytes 32911364 | tf_op jit(solution)/shard_map/while/body/eval_jaxpr/hqk,qhd->khd/dot_general | solution.py:168
  656.4 18.1 %multiply_reduce_fusion.3 = (f32[6,512]{1,0:T(8,128)S(1)}, f32[6,512,2048]{2,1,0:T(8,128)}) fusion(f32[6,512,2048]{2,1,0:T(8,128)} %fusion.140, f32[6,512]{1,0:T(8,128)S(1)} %dynamic-slice_bitcast_fusion.2, pred[512,2048]{1,0:T(8,128)(4,1)S(1)} %broadcast_compare_fusion.5, bf16[2048,6,64]{0,2,1:T(8,128)(2,1)} %get-tuple-element.510, ...), kind=kOutput, calls=%fused_computation.18.clone.1 | convolution fusion | flops 836760576 | bytes 53370884 | tf_op jit(solution)/shard_map/while/body/eval_jaxpr/qhd,khd->hqk/dot_general | solution.py:174
  674.5 21.3 %multiply_convert_fusion.3 = bf16[6,512,2048]{2,1,0:T(8,128)(2,1)} fusion(f32[6,512,2048]{2,1,0:T(8,128)} %get-tuple-element.445, f32[6,512,2048]{2,1,0:T(8,128)} %fusion.140, f32[6,512]{1,0:T(8,128)S(1)} %get-tuple-element.446, f32[6,512]{1,0:T(8,128)S(1)} %dynamic-slice_bitcast_fusion.2, pred[512,2048]{1,0:T(8,128)(4,1)S(1)} %broadcast_compare_fusion.5), kind=kLoop, calls=%fused_computation.17.clone.1 | loop fusion | flops 37748736 | bytes 63987712 | tf_op jit(solution)/shard_map/while/body/eval_jaxpr/convert_element_type | solution.py:178
  695.8 9.3 fusion.141
  705.0 9.6 bitcast_add_fusion.4
  715.0 3.8 copy.52
  732.9 8.9 bitcast_convert_fusion
  741.9 9.8 fusion.81
  751.7 9.1 fusion.82
  764.5 5.8 fusion.66
  777.7 3.4 all-reduce.2
  781.1 81.8 %all-reduce = (f32[2,768]{1,0:T(2,128)}, f32[4,768]{1,0:T(4,128)}, f32[2,384]{1,0:T(2,128)}, f32[1536]{0:T(1024)}) all-reduce(f32[2,768]{1,0:T(2,128)S(1)} %get-tuple-element.302, f32[4,768]{1,0:T(4,128)S(1)} %get-tuple-element.303, f32[2,384]{1,0:T(2,128)S(1)} %pad_maximum_fusion.6, ...), channel_id=1, replica_groups=mesh['dp'=16,'mp'=2] {'dp'}, use_global_device_ids=true, to_apply=%region_30.31 | all-reduce | flops 6912 | bytes 55296 | tf_op jit(solution)/shard_map/psum | solution.py:12
  862.9 4.1 add_add_fusion.2
  867.0 303.1 %all-reduce.5.cloned.1.call-done = (f32[3,768,384]{1,2,0:T(8,128)}, f32[384,768]{1,0:T(8,128)}, f32[768,1536]{1,0:T(8,128)}, f32[1536,768]{1,0:T(8,128)}) async-done(((f32[3,768,384]{1,2,0:T(8,128)}, f32[384,768]{1,0:T(8,128)}, f32[768,1536]{1,0:T(8,128)}, f32[1536,768]{1,0:T(8,128)}), (f32[3,768,384]{1,2,0:T(8,128)}, f32[384,768]{1,0:T(8,128)}, f32[768,1536]{1,0:T(8,128)}, ...) | async-done | bytes 14155792 | tf_op jit(solution)/shard_map/psum | solution.py:240
  1170.1 5.2 copy.57
  1176.4 5.5 copy.92
  (237 shorter events, 88.1 us)
Async XLA Ops:
  7.2 275.3 %copy-start = (bf16[768,1536]{1,0:T(8,128)(2,1)S(1)}, bf16[768,1536]{1,0:T(8,128)(2,1)}, u32[]{:S(2)}) copy-start(bf16[768,1536]{1,0:T(8,128)(2,1)} %param.25) | copy-start | bytes 7077892
  7.2 4.6 copy-start.39
  7.2 5.2 copy-start.37
  7.2 22.6 %all-gather.5.cloned.1.call-start = ((), (), s32[]{:S(2)}) async-start(), calls=%async_computation.4 | async-start | bytes 4718592 | tf_op jit(solution)/shard_map/all_gather | solution.py:83
  7.3 5.8 copy-start.3
  9.1 3.9 copy-start.22
  9.1 5.8 copy-start.41
  9.1 6.3 copy-start.40
  11.8 1.3 copy-start.27
  14.8 211.6 %reduce-scatter.5.cloned.1.call-start = ((), (), s32[]{:S(2)}) async-start(), calls=%async_computation.5 | async-start | bytes 4718592 | tf_op jit(solution)/shard_map/reduce_scatter | solution.py:112
  61.6 12.1 %copy-start.7 = (bf16[2048,6,64]{0,2,1:T(8,128)(2,1)S(1)}, bf16[2048,6,64]{0,2,1:T(8,128)(2,1)}, u32[]{:S(2)}) copy-start(bf16[2048,6,64]{0,2,1:T(8,128)(2,1)} %get-tuple-element.472) | copy-start | bytes 4718596 | tf_op jit(solution)/shard_map/while
  61.6 12.1 %copy-start.13 = (bf16[4,512,6,64]{1,3,2,0:T(8,128)(2,1)S(1)}, bf16[4,512,6,64]{1,3,2,0:T(8,128)(2,1)}, u32[]{:S(2)}) copy-start(bf16[4,512,6,64]{1,3,2,0:T(8,128)(2,1)} %get-tuple-element.457) | copy-start | bytes 4718596 | tf_op jit(solution)/shard_map/while
  85.4 1.1 copy-start.14
  101.5 12.1 %copy-start.7 = (bf16[2048,6,64]{0,2,1:T(8,128)(2,1)S(1)}, bf16[2048,6,64]{0,2,1:T(8,128)(2,1)}, u32[]{:S(2)}) copy-start(bf16[2048,6,64]{0,2,1:T(8,128)(2,1)} %get-tuple-element.472) | copy-start | bytes 4718596 | tf_op jit(solution)/shard_map/while
  101.5 12.1 %copy-start.13 = (bf16[4,512,6,64]{1,3,2,0:T(8,128)(2,1)S(1)}, bf16[4,512,6,64]{1,3,2,0:T(8,128)(2,1)}, u32[]{:S(2)}) copy-start(bf16[4,512,6,64]{1,3,2,0:T(8,128)(2,1)} %get-tuple-element.457) | copy-start | bytes 4718596 | tf_op jit(solution)/shard_map/while
  125.2 1.1 copy-start.14
  141.3 12.1 %copy-start.7 = (bf16[2048,6,64]{0,2,1:T(8,128)(2,1)S(1)}, bf16[2048,6,64]{0,2,1:T(8,128)(2,1)}, u32[]{:S(2)}) copy-start(bf16[2048,6,64]{0,2,1:T(8,128)(2,1)} %get-tuple-element.472) | copy-start | bytes 4718596 | tf_op jit(solution)/shard_map/while
  141.3 12.1 %copy-start.13 = (bf16[4,512,6,64]{1,3,2,0:T(8,128)(2,1)S(1)}, bf16[4,512,6,64]{1,3,2,0:T(8,128)(2,1)}, u32[]{:S(2)}) copy-start(bf16[4,512,6,64]{1,3,2,0:T(8,128)(2,1)} %get-tuple-element.457) | copy-start | bytes 4718596 | tf_op jit(solution)/shard_map/while
  165.1 1.1 copy-start.14
  181.2 12.1 %copy-start.7 = (bf16[2048,6,64]{0,2,1:T(8,128)(2,1)S(1)}, bf16[2048,6,64]{0,2,1:T(8,128)(2,1)}, u32[]{:S(2)}) copy-start(bf16[2048,6,64]{0,2,1:T(8,128)(2,1)} %get-tuple-element.472) | copy-start | bytes 4718596 | tf_op jit(solution)/shard_map/while
  181.2 12.1 %copy-start.13 = (bf16[4,512,6,64]{1,3,2,0:T(8,128)(2,1)S(1)}, bf16[4,512,6,64]{1,3,2,0:T(8,128)(2,1)}, u32[]{:S(2)}) copy-start(bf16[4,512,6,64]{1,3,2,0:T(8,128)(2,1)} %get-tuple-element.457) | copy-start | bytes 4718596 | tf_op jit(solution)/shard_map/while
  205.0 1.1 copy-start.14
  206.3 4.3 copy-start.47
  209.4 1.2 copy-start.15
  214.1 12.3 %copy-start.21 = (f32[768]{0:T(1024)S(1)}, f32[768]{0:T(1024)}, u32[]{:S(2)}) copy-start(f32[768]{0:T(1024)} %get-tuple-element.249) | copy-start | bytes 9220
  214.2 68.3 %all-gather.7.cloned.1.call-start = ((), (), s32[]{:S(2)}) async-start(), calls=%async_computation.6 | async-start | bytes 4718592 | tf_op jit(solution)/shard_map/all_gather | solution.py:120
  226.4 2.6 copy-start.4
  226.4 2.8 copy-start.8
  226.4 3.7 copy-start.26
  226.4 3.7 copy-start.34
  230.1 2.8 copy-start.42
  232.2 50.3 %copy-start.48 = (f32[1536]{0:T(1024)S(1)}, f32[1536]{0:T(1024)}, u32[]{:S(2)}) copy-start(f32[1536]{0:T(1024)} %param.26) | copy-start | bytes 18436
  232.2 64.0 %all-gather.9.cloned.1.call-start = ((), (), s32[]{:S(2)}) async-start(), calls=%async_computation.8 | async-start | bytes 4718592 | tf_op jit(solution)/shard_map/all_gather | solution.py:133
  282.4 54.2 %reduce-scatter.9.cloned.1.call-start = ((), (), s32[]{:S(2)}) async-start(), calls=%async_computation.9 | async-start | bytes 4718592 | tf_op jit(solution)/shard_map/reduce_scatter | solution.py:144
  315.6 2.6 copy-start.49
  324.6 1.7 copy-start.46
  324.7 21.7 %reduce-scatter.7.cloned.1.call-start = ((), (), s32[]{:S(2)}) async-start(), calls=%async_computation.7 | async-start | bytes 4718592 | tf_op jit(solution)/shard_map/reduce_scatter | solution.py:125
  335.9 1.4 copy-start.5
  336.0 32.4 %all-gather.11.cloned.1.call-start = ((), (), s32[]{:S(2)}) async-start(), calls=%async_computation.10 | async-start | bytes 4718592 | tf_op jit(solution)/shard_map/all_gather | solution.py:154
  337.4 3.9 copy-start.12
  341.2 5.1 copy-start.31
  351.9 1.7 copy-start.9
  354.9 417.8 %reduce-scatter.11.cloned.1.call-start = ((), (), s32[]{:S(2)}) async-start(), calls=%async_computation.11 | async-start | bytes 4718592 | tf_op jit(solution)/shard_map/reduce_scatter | solution.py:215
  377.3 4.4 copy-start.2
  721.6 5.0 copy-start.10
  741.8 428.3 %all-reduce.5.cloned.1.call-start = ((), (), s32[]{:S(2)}) async-start(), calls=%async_computation.12 | async-start | bytes 28311552 | tf_op jit(solution)/shard_map/psum | solution.py:240
  741.9 9.8 copy-start.44
  751.7 9.1 copy-start.16
  751.7 9.1 copy-start.45
  760.7 2.4 copy-start.17
  760.8 2.4 copy-start.18
  760.8 2.4 copy-start.19
  760.8 3.7 copy-start.43
  770.3 2.5 copy-start.6
  770.3 2.5 copy-start.23
  770.3 2.5 copy-start.25
  770.3 5.1 copy-start.30
  770.3 5.1 copy-start.28
  772.7 8.4 copy-start.38
  772.8 2.7 copy-start.11
  1170.1 5.3 copy-start.20
  1175.4 6.5 slice-start
  1176.4 5.5 slice-start.1
  1176.4 7.7 copy-start.1
  (6 other events, 4.0 us)
Sparse Core Ops, SparseCore 0:
  15.0 14.8 all-gather.4
  214.3 12.0 reduce-scatter.4
  232.3 13.3 all-gather.6
  282.5 7.9 all-gather.8
  324.8 6.7 reduce-scatter.8
  336.1 10.2 reduce-scatter.6
  355.1 13.2 all-gather.10
  742.0 12.0 reduce-scatter.10
  770.4 399.6 all-reduce.4
